TPU v7x, 32 devices: a whole 2x2x4 slice. The times are simulated.
32 devices in a mesh: frow: 16 (over z, y, core), fcol: 2 (over x).
Axes of the slice: x: 2, y: 2, z: 4, core: 2. Of those that a mesh axis runs over, the one named last changes fastest.
Arguments:
- face_input: bfloat16 [12, 64, 64, 256], P(None, 'frow', 'fcol'), may hold values from -6 to 6
- kernel: bfloat16 [3, 3, 256, 256], replicated, may hold values from -0.125 to 0.125
- convolution_bias: float32 [256], replicated, may hold values from -3 to 3
- upstream: bfloat16 [12, 64, 64, 256], P(None, 'frow', 'fcol'), may hold values from -6 to 6
- adjacency: int32 [12, 4, 3], replicated, may hold values from 0 to 11, as said below
Outputs:
- activation: bfloat16 [12, 64, 64, 256], P(None, 'frow', 'fcol')
- input_gradient: bfloat16 [12, 64, 64, 256], P(None, 'frow', 'fcol')
- kernel_grad: float32 [3, 3, 256, 256], replicated
- bias_grad: float32 [256], replicated
Inputs may be any that keep to these rules, and one draw needn't show every extreme that they name: adjacency[f, s] = (g, t, r): side s of face f (0 top, 1 bottom, 2 left, 3 right) borders side t of face g; t is 0 or 1 exactly when s is; r = 1 when positions along the seam run in opposite directions, else 0; the relation is symmetric, adjacency[g, t] = (f, s, r), and no side borders itself.
All inputs are finite; a program needn't handle non-finite values.
Results may differ from a plain program's by a relative error of at most 0.018.
Values may be sent and summed in bfloat16 or wider, within the bound.
No kernel may reach another device: no remote copies, remote signals or barrier semaphores. Data moves between devices by JAX's collectives and lax.ppermute only.
A program may use at most 128 MiB of HBM per device.

v0:
```python
import math
import jax
import jax.numpy as jnp
from jax import lax
from jax.sharding import PartitionSpec as P

DILATION_STEP = 2
half_root = 0.7071067811865476
density_scale = 0.3989422804014327


def from_partner(value, axis, distance):
    return lax.ppermute(value, axis, [(i, i ^ 1 << distance) for i in range(lax.axis_size(axis))])


def with_halo(block, sides, width):
    for axis, dim in sides:
        count = lax.axis_size(axis)
        forward = [(i, i + 1) for i in range(count - 1)]
        forward.append((count - 1, 0))
        backward = [(target, source) for source, target in forward]
        low = lax.ppermute(
            lax.slice_in_dim(block, block.shape[dim] - width, None, axis=dim), axis, forward
        )
        high = lax.ppermute(lax.slice_in_dim(block, 0, width, axis=dim), axis, backward)
        block = jnp.concatenate([low, block, high], axis=dim)
    return block


def gelu_value(value):
    return 0.5 * value * (1.0 + jax.scipy.special.erf(value * half_root))


def gelu_slope(value):
    return (
        0.5 * (1.0 + jax.scipy.special.erf(value * half_root))
        + value * jnp.exp(-0.5 * value * value) * density_scale
    )


def pick_table(entries, side_near, face_count):
    same_side = (entries[:, 1] == side_near).astype(jnp.int32)
    slot_index = (2 * entries[:, 2] + same_side) * face_count + entries[:, 0]
    return (slot_index[:, None] == jnp.arange(4 * face_count, dtype=jnp.int32)[None, :]).astype(
        jnp.bfloat16
    )


def reflect(row_band, col_band, returning):
    col_bits = lax.axis_size("fcol").bit_length() - 1
    all_bits = (lax.axis_size("frow") * lax.axis_size("fcol")).bit_length() - 1
    for bit_index in range(all_bits):
        moving = row_band if bit_index < col_bits else col_band
        if returning:
            moved = from_partner(moving, ("frow", "fcol"), bit_index)
        else:
            moved = from_partner(moving, ("frow", "fcol"), bit_index)
        if bit_index < col_bits:
            row_band = moved
        else:
            col_band = moved
    return (row_band, col_band)


def fold_border(extended, along, cells, inner_size):
    middle = lax.slice_in_dim(extended, 2 * cells, 2 * cells + inner_size, axis=along)
    before = lax.slice_in_dim(extended, 0, cells, axis=along)
    after_rim = lax.slice_in_dim(
        extended, inner_size + 3 * cells, inner_size + 4 * cells, axis=along
    )
    lead_pads = [(0, 0)] * extended.ndim
    tail_pads = [(0, 0)] * extended.ndim
    lead_pads[along] = (0, inner_size - cells)
    tail_pads[along] = (inner_size - cells, 0)
    return middle + jnp.pad(before, lead_pads) + jnp.pad(after_rim, tail_pads)


def local(face_input, kernel, convolution_bias, upstream, adjacency):
    face_count = face_input.shape[0]
    tile_rows = face_input.shape[1]
    tile_cols = face_input.shape[2]
    dilation_step = DILATION_STEP
    height = tile_rows + 2 * dilation_step
    breadth = tile_cols + 2 * dilation_step
    at_top = lax.axis_index("frow") == 0
    at_bottom = lax.axis_index("frow") == lax.axis_size("frow") - 1
    at_left = lax.axis_index("fcol") == 0
    at_right = lax.axis_index("fcol") == lax.axis_size("fcol") - 1
    column_index = jnp.arange(breadth)
    keep_cols = jnp.logical_not(
        at_left & (column_index < dilation_step)
        | at_right & (column_index >= tile_cols + dilation_step)
    )
    row_index = jnp.arange(height)
    keep_rows = jnp.logical_not(
        at_top & (row_index < dilation_step) | at_bottom & (row_index >= tile_rows + dilation_step)
    )
    padded_input = with_halo(face_input, (("frow", 1), ("fcol", 2)), dilation_step)
    row_wrap = jnp.where(
        at_top, padded_input[:, :dilation_step], padded_input[:, tile_rows + dilation_step :]
    )
    row_own = jnp.where(
        at_top,
        padded_input[:, dilation_step : 2 * dilation_step],
        padded_input[:, tile_rows : tile_rows + dilation_step],
    )
    col_wrap = jnp.where(
        at_left, padded_input[:, :, :dilation_step], padded_input[:, :, tile_cols + dilation_step :]
    )
    col_own = jnp.where(
        at_left,
        padded_input[:, :, dilation_step : 2 * dilation_step],
        padded_input[:, :, tile_cols : tile_cols + dilation_step],
    )
    row_send = jnp.concatenate([row_wrap, row_own], 1)
    col_send = jnp.concatenate([col_wrap, col_own], 2)
    far_rows, far_cols = reflect(row_send, col_send, False)
    row_pick = pick_table(
        jnp.where(at_top, adjacency[:, 0], adjacency[:, 1]), jnp.where(at_top, 0, 1), face_count
    )
    col_pick = pick_table(
        jnp.where(at_left, adjacency[:, 2], adjacency[:, 3]), jnp.where(at_left, 2, 3), face_count
    )
    row_cands = jnp.concatenate(
        [
            row_wrap,
            jnp.flip(row_own, 1),
            jnp.flip(far_rows[:, :dilation_step], 2),
            jnp.flip(far_rows[:, dilation_step:], (1, 2)),
        ],
        0,
    )
    row_halo = jnp.einsum("fk,kdwc->fdwc", row_pick, row_cands, preferred_element_type=jnp.float32)
    row_halo = jnp.where(keep_cols[None, None, :, None], row_halo, 0.0).astype(jnp.bfloat16)
    top_rim = jnp.where(at_top, row_halo, padded_input[:, :dilation_step])
    bottom_rim = jnp.where(at_bottom, row_halo, padded_input[:, tile_rows + dilation_step :])
    padded_input = jnp.concatenate(
        [top_rim, padded_input[:, dilation_step : tile_rows + dilation_step], bottom_rim], 1
    )
    col_cands = jnp.concatenate(
        [
            col_wrap,
            jnp.flip(col_own, 2),
            jnp.flip(far_cols[:, :, :dilation_step], 1),
            jnp.flip(far_cols[:, :, dilation_step:], (1, 2)),
        ],
        0,
    )
    col_halo = jnp.einsum("fk,kadc->fadc", col_pick, col_cands, preferred_element_type=jnp.float32)
    col_halo = jnp.where(keep_rows[None, :, None, None], col_halo, 0.0).astype(jnp.bfloat16)
    left_rim = jnp.where(at_left, col_halo, padded_input[:, :, :dilation_step])
    right_rim = jnp.where(at_right, col_halo, padded_input[:, :, tile_cols + dilation_step :])
    padded_input = jnp.concatenate(
        [left_rim, padded_input[:, :, dilation_step : tile_cols + dilation_step], right_rim], 2
    )
    random_values = ("NHWC", "HWIO", "NHWC")
    preactivation = (
        lax.conv_general_dilated(
            padded_input,
            kernel,
            (1, 1),
            "VALID",
            rhs_dilation=(dilation_step, dilation_step),
            dimension_numbers=random_values,
            preferred_element_type=jnp.float32,
        )
        + convolution_bias
    )
    activation = gelu_value(preactivation).astype(jnp.bfloat16)
    preactivation_gradient = (upstream.astype(jnp.float32) * gelu_slope(preactivation)).astype(
        jnp.bfloat16
    )
    tap_list = []
    for kernel_row_offset in range(3):
        for kernel_column_offset in range(3):
            input_window = padded_input[
                :,
                kernel_row_offset * dilation_step : kernel_row_offset * dilation_step + tile_rows,
                kernel_column_offset * dilation_step : kernel_column_offset * dilation_step
                + tile_cols,
            ]
            tap_list.append(
                lax.dot_general(
                    input_window,
                    preactivation_gradient,
                    (((0, 1, 2), (0, 1, 2)), ((), ())),
                    preferred_element_type=jnp.float32,
                )
            )
    kernel_local = jnp.stack(tap_list, 0).reshape(kernel.shape)
    bias_local = jnp.sum(preactivation_gradient.astype(jnp.float32), axis=(0, 1, 2))
    kernel_total, bias_total = lax.psum((kernel_local, bias_local), ("frow", "fcol"))
    scale = 1.0 / math.sqrt(
        face_count * tile_rows * lax.axis_size("frow") * tile_cols * lax.axis_size("fcol")
    )
    kernel_grad = kernel_total * scale
    bias_grad = bias_total * scale
    rotated_strip = jnp.transpose(jnp.flip(kernel, (0, 1)), (0, 1, 3, 2))
    twice = 2 * dilation_step
    padded_gradient = lax.conv_general_dilated(
        preactivation_gradient,
        rotated_strip,
        (1, 1),
        ((twice, twice), (twice, twice)),
        rhs_dilation=(dilation_step, dilation_step),
        dimension_numbers=random_values,
        preferred_element_type=jnp.float32,
    ).astype(jnp.bfloat16)
    row_seam = jnp.where(
        at_top, padded_gradient[:, :dilation_step], padded_gradient[:, tile_rows + dilation_step :]
    )
    row_seam = jnp.where(keep_cols[None, None, :, None], row_seam, jnp.zeros_like(row_seam))
    row_split = jnp.einsum("fk,fdwc->kdwc", row_pick, row_seam, preferred_element_type=jnp.float32)
    row_split = row_split.reshape((4, face_count) + row_split.shape[1:])
    col_seam = jnp.where(
        at_left,
        padded_gradient[:, :, :dilation_step],
        padded_gradient[:, :, tile_cols + dilation_step :],
    )
    col_seam = jnp.where(keep_rows[None, :, None, None], col_seam, jnp.zeros_like(col_seam))
    col_split = jnp.einsum("fk,fadc->kadc", col_pick, col_seam, preferred_element_type=jnp.float32)
    col_split = col_split.reshape((4, face_count) + col_split.shape[1:])
    row_far_grad = jnp.concatenate(
        [jnp.flip(row_split[2], 2), jnp.flip(row_split[3], (1, 2))], 1
    ).astype(jnp.bfloat16)
    col_far_grad = jnp.concatenate(
        [jnp.flip(col_split[2], 1), jnp.flip(col_split[3], (1, 2))], 2
    ).astype(jnp.bfloat16)
    row_back, col_back = reflect(row_far_grad, col_far_grad, True)
    wrap_rows = row_split[0] + row_back[:, :dilation_step].astype(jnp.float32)
    own_rows = jnp.flip(row_split[1], 1) + row_back[:, dilation_step:].astype(jnp.float32)
    wrap_cols = col_split[0] + col_back[:, :, :dilation_step].astype(jnp.float32)
    own_cols = jnp.flip(col_split[1], 2) + col_back[:, :, dilation_step:].astype(jnp.float32)
    gathered = padded_gradient.astype(jnp.float32)
    middle_rows = gathered[:, dilation_step : tile_rows + dilation_step]
    middle_rows = middle_rows + jnp.pad(
        jnp.where(at_top, own_rows, 0.0), ((0, 0), (0, tile_rows - dilation_step), (0, 0), (0, 0))
    )
    middle_rows = middle_rows + jnp.pad(
        jnp.where(at_bottom, own_rows, 0.0),
        ((0, 0), (tile_rows - dilation_step, 0), (0, 0), (0, 0)),
    )
    top_grad = jnp.where(at_top, wrap_rows, gathered[:, :dilation_step])
    bottom_grad = jnp.where(at_bottom, wrap_rows, gathered[:, tile_rows + dilation_step :])
    gathered = jnp.concatenate([top_grad, middle_rows, bottom_grad], 1)
    middle_cols = gathered[:, :, dilation_step : tile_cols + dilation_step]
    middle_cols = middle_cols + jnp.pad(
        jnp.where(at_left, own_cols, 0.0), ((0, 0), (0, 0), (0, tile_cols - dilation_step), (0, 0))
    )
    middle_cols = middle_cols + jnp.pad(
        jnp.where(at_right, own_cols, 0.0), ((0, 0), (0, 0), (tile_cols - dilation_step, 0), (0, 0))
    )
    left_grad = jnp.where(at_left, wrap_cols, gathered[:, :, :dilation_step])
    right_grad = jnp.where(at_right, wrap_cols, gathered[:, :, tile_cols + dilation_step :])
    gathered = jnp.concatenate([left_grad, middle_cols, right_grad], 2)
    returned = with_halo(
        gathered.astype(jnp.bfloat16), (("frow", 1), ("fcol", 2)), dilation_step
    ).astype(gathered.dtype)
    folded = fold_border(returned, 1, dilation_step, tile_rows)
    folded = fold_border(folded, 2, dilation_step, tile_cols)
    input_gradient = folded.astype(jnp.bfloat16)
    return (activation, input_gradient, kernel_grad, bias_grad)


def solution(mesh):
    return jax.shard_map(
        local,
        mesh=mesh,
        in_specs=(P(None, "frow", "fcol", None), P(), P(), P(None, "frow", "fcol", None), P()),
        out_specs=(P(None, "frow", "fcol", None), P(None, "frow", "fcol", None), P(), P()),
        check_vma=False,
    )
```

profile of v0, /device:TPU:0, one launch (start us, length us, event | category | flops | bytes accessed | tf_op | source)
XLA Modules:
  0.0 288.5 jit_solution(14397074329144345583)
XLA Ops:
  9.5 5.1 %collective-permute-start.1 = (bf16[12,2,32,256]{3,0,2,1:T(8,128)(2,1)S(1)}, bf16[12,2,32,256]{3,0,2,1:T(8,128)(2,1)}, u32[]{:S(2)}, u32[]{:S(2)}) collective-permute-start(bf16[12,2,32,256]{3,0,2,1:T(8,128)(2,1)S(1)} %copy.171), channel_id=1, source_target_pairs={{2,0},{4,2},{6,4},{8,6},{10,8},{12,10},{14,12},{16,14},{18,16},{20... | collective-permute-start | bytes 1179656 | tf_op jit(solution)/shard_map/ppermute | solution.py:25
  14.6 6.8 %collective-permute-done = bf16[12,2,32,256]{3,0,2,1:T(8,128)(2,1)} collective-permute-done((bf16[12,2,32,256]{3,0,2,1:T(8,128)(2,1)S(1)}, bf16[12,2,32,256]{3,0,2,1:T(8,128)(2,1)}, u32[]{:S(2)}, u32[]{:S(2)}) %collective-permute-start) | collective-permute-done | bytes 393248 | tf_op jit(solution)/shard_map/ppermute | solution.py:22
  25.4 2.0 collective-permute-start.3
  27.5 2.9 %collective-permute-done.3 = bf16[12,8,2,256]{3,0,2,1:T(8,128)(2,1)S(1)} collective-permute-done((bf16[12,8,2,256]{3,0,2,1:T(8,128)(2,1)S(1)}, bf16[12,8,2,256]{3,0,2,1:T(8,128)(2,1)S(1)}, u32[]{:S(2)}, u32[]{:S(2)}) %collective-permute-start.3) | collective-permute-done | bytes 98336 | tf_op jit(solution)/shard_map/ppermute | solution.py:25
  30.4 2.7 collective-permute-done.2
  33.1 2.0 collective-permute-start.4
  35.1 1.9 pad_maximum_fusion.1
  43.2 6.7 %collective-permute-done.5 = bf16[12,8,4,256]{3,0,2,1:T(8,128)(2,1)S(1)} collective-permute-done((bf16[12,8,4,256]{3,0,2,1:T(8,128)(2,1)S(1)}, bf16[12,8,4,256]{3,0,2,1:T(8,128)(2,1)S(1)}, u32[]{:S(2)}, u32[]{:S(2)}) %collective-permute-start.5) | collective-permute-done | bytes 196640 | tf_op jit(solution)/shard_map/ppermute | solution.py:13
  51.5 6.3 %collective-permute-done.6 = bf16[12,8,4,256]{3,0,2,1:T(8,128)(2,1)S(1)} collective-permute-done((bf16[12,8,4,256]{3,0,2,1:T(8,128)(2,1)S(1)}, bf16[12,8,4,256]{3,0,2,1:T(8,128)(2,1)S(1)}, u32[]{:S(2)}, u32[]{:S(2)}) %collective-permute-start.6) | collective-permute-done | bytes 196640 | tf_op jit(solution)/shard_map/ppermute | solution.py:13
  57.7 2.8 collective-permute-start.7
  64.4 7.3 %collective-permute-done.7 = bf16[12,8,4,256]{3,0,2,1:T(8,128)(2,1)} collective-permute-done((bf16[12,8,4,256]{3,0,2,1:T(8,128)(2,1)S(1)}, bf16[12,8,4,256]{3,0,2,1:T(8,128)(2,1)}, u32[]{:S(2)}, u32[]{:S(2)}) %collective-permute-start.7) | collective-permute-done | bytes 196640 | tf_op jit(solution)/shard_map/ppermute | solution.py:13
  73.4 3.0 %fusion.111 = (bf16[12,2,36,256]{3,1,2,0:T(2,128)(2,1)S(1)}, bf16[12,2,36,256]{3,1,2,0:T(2,128)(2,1)}) fusion(bf16[12,4,36,256]{3,1,2,0:T(4,128)(2,1)} %collective-permute-done.8), kind=kLoop, calls=%fused_computation.185 | loop fusion | bytes 1769472 | tf_op jit(solution)/shard_map/slice | solution.py:128
  77.3 1.9 rev.54
  83.1 2.7 broadcast_select_fusion.1
  88.5 2.1 pad_maximum_fusion.5
  90.7 2.8 fusion.5
  93.5 2.6 convert_reduce_fusion
  96.1 8.3 %fusion.115 = (f32[12,8,36,256]{3,0,2,1:T(8,128)}, bf16[12,8,36,256]{3,0,2,1:T(8,128)(2,1)S(1)}) fusion(bf16[3,3,256,256]{3,2,1,0:T(8,128)(2,1)S(1)} %copy-done, bf16[12,4,32,256]{3,2,1,0:T(8,128)(2,1)S(1)} %get-tuple-element.21), kind=kOutput, calls=%fused_computation.189 | convolution fusion | flops 1813708800 | bytes 7274496 | tf_op jit(solution)/shard_map/conv_general_dilated | solution.py:200
  104.8 2.6 fusion.60
  111.6 2.0 fusion.108
  119.7 6.2 %collective-permute-done.10 = bf16[12,8,4,256]{3,0,2,1:T(8,128)(2,1)S(1)} collective-permute-done((bf16[12,8,4,256]{3,0,2,1:T(8,128)(2,1)}, bf16[12,8,4,256]{3,0,2,1:T(8,128)(2,1)S(1)}, u32[]{:S(2)}, u32[]{:S(2)}) %collective-permute-start.10) | collective-permute-done | bytes 196640 | tf_op jit(solution)/shard_map/ppermute | solution.py:13
  127.7 5.8 %collective-permute-done.11 = bf16[12,8,4,256]{3,0,2,1:T(8,128)(2,1)S(1)} collective-permute-done((bf16[12,8,4,256]{3,0,2,1:T(8,128)(2,1)S(1)}, bf16[12,8,4,256]{3,0,2,1:T(8,128)(2,1)S(1)}, u32[]{:S(2)}, u32[]{:S(2)}) %collective-permute-start.11) | collective-permute-done | bytes 196640 | tf_op jit(solution)/shard_map/ppermute | solution.py:13
  133.6 2.4 collective-permute-start.12
  137.2 12.1 %collective-permute-done.12 = bf16[12,8,4,256]{3,0,2,1:T(8,128)(2,1)S(1)} collective-permute-done((bf16[12,8,4,256]{3,0,2,1:T(8,128)(2,1)S(1)}, bf16[12,8,4,256]{3,0,2,1:T(8,128)(2,1)S(1)}, u32[]{:S(2)}, u32[]{:S(2)}) %collective-permute-start.12) | collective-permute-done | bytes 196640 | tf_op jit(solution)/shard_map/ppermute | solution.py:13
  149.4 2.2 fusion.110
  151.7 3.5 %slice_select_fusion.3 = (f32[12,2,36,256]{3,0,2,1:T(8,128)S(1)}, f32[12,2,36,256]{3,0,2,1:T(8,128)S(1)}, f32[12,2,36,256]{3,0,2,1:T(8,128)S(1)}) fusion(f32[12,8,36,256]{3,0,2,1:T(8,128)} %get-tuple-element.70, f32[48,2,36,256]{3,0,2,1:T(8,128)} %fusion.60, bf16[12,2,36,256]{3,1,2,0:T(2,128)(2,1)S(1)} %get-tuple-element.57, pred[]{:T(512)S(6)} %eq.57, ...), kind=kLoop, calls=%fused_computation.53 | loop fusion | flops 884736 | bytes 6635522 | tf_op jit(solution)/shard_map/jit(_where)/select_n | solution.py:243
  158.7 4.1 %collective-permute-start.15 = (bf16[12,2,36,256]{3,1,2,0:T(2,128)(2,1)}, bf16[12,2,36,256]{3,1,2,0:T(2,128)(2,1)S(1)}, u32[]{:S(2)}, u32[]{:S(2)}) collective-permute-start(bf16[12,2,36,256]{3,1,2,0:T(2,128)(2,1)} %copy.103), channel_id=1, source_target_pairs={{2,0},{4,2},{6,4},{8,6},{10,8},{12,10},{14,12},{16,14},{18,16},{20... | collective-permute-start | bytes 1327112 | tf_op jit(solution)/shard_map/ppermute | solution.py:25
  164.1 42.6 %psum.15 = f32[256]{0:T(256)S(1)} all-reduce(f32[256]{0:T(256)S(1)} %get-tuple-element.20), channel_id=1, replica_groups=mesh['frow'=16,'fcol'=2] {'frow','fcol'}, use_global_device_ids=true, to_apply=%region_2.3 | all-reduce | flops 256 | bytes 2048 | tf_op jit(solution)/shard_map/psum | solution.py:192
  209.4 2.3 collective-permute-start.16
  211.7 60.8 %all-reduce.8.cloned.1.call-done = f32[3,3,256,256]{3,2,1,0:T(8,128)} async-done(((f32[3,3,256,256]{3,2,1,0:T(8,128)}), f32[3,3,256,256]{3,2,1,0:T(8,128)}) %all-reduce.8.cloned.1.call-update) | async-done | bytes 2359312 | tf_op jit(solution)/shard_map/psum | solution.py:192
  272.5 3.3 %broadcast_multiply_fusion = f32[3,3,256,256]{3,2,1,0:T(8,128)} fusion(f32[3,3,256,256]{3,2,1,0:T(8,128)} %all-reduce.8.cloned.1.call-done), kind=kLoop, calls=%fused_computation.57 | loop fusion | flops 589824 | bytes 4718592 | tf_op jit(solution)/shard_map/mul | solution.py:196
  275.7 2.9 %maximum_convert_fusion = f32[12,12,40,256]{3,0,2,1:T(8,128)S(1)} fusion(bf16[12,12,2,256]{3,0,2,1:T(8,128)(2,1)} %collective-permute-done.17, bf16[12,2,36,256]{3,0,2,1:T(8,128)(2,1)S(1)} %copy.105, bf16[12,8,2,256]{3,0,2,1:T(8,128)(2,1)S(1)} %get-tuple-element.25, bf16[12,8,32,256]{3,0,2,1:T(8,128)(2,1)S(1)} %fusion.1, ...), kind=kLoop, calls=%fused_computation.4 | loop fusion | flops 10321920 | bytes 8847360 | tf_op jit(solution)/shard_map/convert_element_type | solution.py:258
  (142 shorter events, 51.4 us)
Async XLA Ops:
  7.2 83.5 %copy-start = (bf16[3,3,256,256]{3,2,1,0:T(8,128)(2,1)S(1)}, bf16[3,3,256,256]{3,2,1,0:T(8,128)(2,1)}, u32[]{:S(2)}) copy-start(bf16[3,3,256,256]{3,2,1,0:T(8,128)(2,1)} %param.6) | copy-start | bytes 3538948
  7.2 15.3 %copy-start.3 = (bf16[12,4,32,256]{3,2,1,0:T(8,128)(2,1)S(1)}, bf16[12,4,32,256]{3,2,1,0:T(8,128)(2,1)}, u32[]{:S(2)}) copy-start(bf16[12,4,32,256]{3,2,1,0:T(8,128)(2,1)} %param.5) | copy-start | bytes 2359300
  7.2 265.3 %all-reduce.8.cloned.1.call-start = ((), (), s32[]{:S(2)}) async-start(), calls=%async_computation | async-start | bytes 4718592 | tf_op jit(solution)/shard_map/psum | solution.py:192
  8.8 12.6 %collective-permute-start = (bf16[12,2,32,256]{3,0,2,1:T(8,128)(2,1)S(1)}, bf16[12,2,32,256]{3,0,2,1:T(8,128)(2,1)}, u32[]{:S(2)}, u32[]{:S(2)}) collective-permute-start(bf16[12,2,32,256]{3,0,2,1:T(8,128)(2,1)S(1)} %copy.170), channel_id=1, source_target_pairs={{0,2},{2,4},{4,6},{6,8},{8,10},{10,12},{12,14},{14,16},{16,18},{18... | collective-permute-start | bytes 1179656 | tf_op jit(solution)/shard_map/ppermute | solution.py:22
  9.5 17.9 %copy-start.17 = (s32[12,4,3]{0,1,2:T(4,128)S(1)}, s32[12,4,3]{0,1,2:T(4,128)}, u32[]{:S(2)}) copy-start(s32[12,4,3]{0,1,2:T(4,128)} %param.9) | copy-start | bytes 1732
  9.5 13.4 %collective-permute-start.1 = (bf16[12,2,32,256]{3,0,2,1:T(8,128)(2,1)S(1)}, bf16[12,2,32,256]{3,0,2,1:T(8,128)(2,1)}, u32[]{:S(2)}, u32[]{:S(2)}) collective-permute-start(bf16[12,2,32,256]{3,0,2,1:T(8,128)(2,1)S(1)} %copy.171), channel_id=1, source_target_pairs={{2,0},{4,2},{6,4},{8,6},{10,8},{12,10},{14,12},{16,14},{18,16},{20... | collective-permute-start | bytes 1179656 | tf_op jit(solution)/shard_map/ppermute | solution.py:25
  25.4 5.0 %collective-permute-start.3 = (bf16[12,8,2,256]{3,0,2,1:T(8,128)(2,1)S(1)}, bf16[12,8,2,256]{3,0,2,1:T(8,128)(2,1)S(1)}, u32[]{:S(2)}, u32[]{:S(2)}) collective-permute-start(bf16[12,8,2,256]{3,0,2,1:T(8,128)(2,1)S(1)} %get-tuple-element.49), channel_id=1, source_target_pairs={{1,0},{0,1},{3,2},{2,3},{5,4},{4,5},{7,6},{6,7},{9,8},{8,9},{11,10... | collective-permute-start | bytes 294920 | tf_op jit(solution)/shard_map/ppermute | solution.py:25
  27.4 5.7 %collective-permute-start.2 = (bf16[12,8,2,256]{3,0,2,1:T(8,128)(2,1)S(1)}, bf16[12,8,2,256]{3,0,2,1:T(8,128)(2,1)S(1)}, u32[]{:S(2)}, u32[]{:S(2)}) collective-permute-start(bf16[12,8,2,256]{3,0,2,1:T(8,128)(2,1)S(1)} %get-tuple-element.51), channel_id=1, source_target_pairs={{0,1},{1,0},{2,3},{3,2},{4,5},{5,4},{6,7},{7,6},{8,9},{9,8},{10,11... | collective-permute-start | bytes 294920 | tf_op jit(solution)/shard_map/ppermute | solution.py:22
  33.1 8.4 %collective-permute-start.4 = (bf16[12,8,4,256]{3,0,2,1:T(8,128)(2,1)S(1)}, bf16[12,8,4,256]{3,0,2,1:T(8,128)(2,1)S(1)}, u32[]{:S(2)}, u32[]{:S(2)}) collective-permute-start(bf16[12,8,4,256]{3,0,2,1:T(8,128)(2,1)S(1)} %pad_maximum_fusion.12), channel_id=1, source_target_pairs={{0,2},{1,3},{2,0},{3,1},{4,6},{5,7},{6,4},{7,5},{8,10},{9,11},{10,... | collective-permute-start | bytes 589832 | tf_op jit(solution)/shard_map/ppermute | solution.py:13
  37.2 2.9 %copy-start.4 = (bf16[12,2,36,256]{3,0,2,1:T(8,128)(2,1)}, bf16[12,2,36,256]{3,0,2,1:T(8,128)(2,1)S(1)}, u32[]{:S(2)}) copy-start(bf16[12,2,36,256]{3,0,2,1:T(8,128)(2,1)S(1)} %get-tuple-element.38) | copy-start | bytes 1327108
  37.2 4.3 %copy-start.9 = (bf16[12,2,36,256]{3,0,2,1:T(8,128)(2,1)}, bf16[12,2,36,256]{3,0,2,1:T(8,128)(2,1)S(1)}, u32[]{:S(2)}) copy-start(bf16[12,2,36,256]{3,0,2,1:T(8,128)(2,1)S(1)} %get-tuple-element.37) | copy-start | bytes 1327108
  40.1 33.3 %collective-permute-start.8 = (bf16[12,4,36,256]{3,1,2,0:T(4,128)(2,1)}, bf16[12,4,36,256]{3,1,2,0:T(4,128)(2,1)}, u32[]{:S(2)}, u32[]{:S(2)}) collective-permute-start(bf16[12,4,36,256]{3,1,2,0:T(4,128)(2,1)} %copy.94), channel_id=1, source_target_pairs={{0,1},{1,0},{2,3},{3,2},{4,5},{5,4},{6,7},{7,6},{8,9},{9,8},{10,11... | collective-permute-start | bytes 2654216 | tf_op jit(solution)/shard_map/ppermute | solution.py:13
  41.5 8.4 %collective-permute-start.5 = (bf16[12,8,4,256]{3,0,2,1:T(8,128)(2,1)S(1)}, bf16[12,8,4,256]{3,0,2,1:T(8,128)(2,1)S(1)}, u32[]{:S(2)}, u32[]{:S(2)}) collective-permute-start(bf16[12,8,4,256]{3,0,2,1:T(8,128)(2,1)S(1)} %collective-permute-done.4), channel_id=1, source_target_pairs={{0,4},{1,5},{2,6},{3,7},{4,0},{5,1},{6,2},{7,3},{8,12},{9,13},{10,... | collective-permute-start | bytes 589832 | tf_op jit(solution)/shard_map/ppermute | solution.py:13
  43.2 39.9 %copy-start.21 = (pred[36]{0:T(512)(128)(4,1)}, pred[36]{0:T(512)(128)(4,1)S(1)}, u32[]{:S(2)}) copy-start(pred[36]{0:T(512)(128)(4,1)S(1)} %or_not_fusion) | copy-start | bytes 112
  49.9 7.9 %collective-permute-start.6 = (bf16[12,8,4,256]{3,0,2,1:T(8,128)(2,1)S(1)}, bf16[12,8,4,256]{3,0,2,1:T(8,128)(2,1)S(1)}, u32[]{:S(2)}, u32[]{:S(2)}) collective-permute-start(bf16[12,8,4,256]{3,0,2,1:T(8,128)(2,1)S(1)} %collective-permute-done.5), channel_id=1, source_target_pairs={{0,8},{1,9},{2,10},{3,11},{4,12},{5,13},{6,14},{7,15},{8,0},{9,1},... | collective-permute-start | bytes 589832 | tf_op jit(solution)/shard_map/ppermute | solution.py:13
  57.7 14.0 %collective-permute-start.7 = (bf16[12,8,4,256]{3,0,2,1:T(8,128)(2,1)S(1)}, bf16[12,8,4,256]{3,0,2,1:T(8,128)(2,1)}, u32[]{:S(2)}, u32[]{:S(2)}) collective-permute-start(bf16[12,8,4,256]{3,0,2,1:T(8,128)(2,1)S(1)} %collective-permute-done.6), channel_id=1, source_target_pairs={{0,16},{1,17},{2,18},{3,19},{4,20},{5,21},{6,22},{7,23},{8,24},{9,... | collective-permute-start | bytes 589832 | tf_op jit(solution)/shard_map/ppermute | solution.py:13
  90.7 2.8 copy-start.18
  96.1 8.7 %copy-start.22 = (pred[36]{0:T(512)(128)(4,1)S(1)}, pred[36]{0:T(512)(128)(4,1)}, u32[]{:S(2)}) copy-start(pred[36]{0:T(512)(128)(4,1)} %copy-done.21) | copy-start | bytes 112
  104.7 5.2 %copy-start.6 = (f32[48,8,2,256]{3,0,2,1:T(8,128)}, f32[48,8,2,256]{3,0,2,1:T(8,128)S(1)}, u32[]{:S(2)}) copy-start(f32[48,8,2,256]{3,0,2,1:T(8,128)S(1)} %fusion.78) | copy-start | bytes 2359300
  111.5 5.8 %collective-permute-start.9 = (bf16[12,8,4,256]{3,0,2,1:T(8,128)(2,1)S(1)}, bf16[12,8,4,256]{3,0,2,1:T(8,128)(2,1)}, u32[]{:S(2)}, u32[]{:S(2)}) collective-permute-start(bf16[12,8,4,256]{3,0,2,1:T(8,128)(2,1)S(1)} %pad_maximum_fusion.13), channel_id=1, source_target_pairs={{0,2},{1,3},{2,0},{3,1},{4,6},{5,7},{6,4},{7,5},{8,10},{9,11},{10,... | collective-permute-start | bytes 589832 | tf_op jit(solution)/shard_map/ppermute | solution.py:13
  115.4 34.0 %collective-permute-start.13 = (bf16[12,4,36,256]{3,1,2,0:T(4,128)(2,1)}, bf16[12,4,36,256]{3,1,2,0:T(4,128)(2,1)}, u32[]{:S(2)}, u32[]{:S(2)}) collective-permute-start(bf16[12,4,36,256]{3,1,2,0:T(4,128)(2,1)} %copy.99), channel_id=1, source_target_pairs={{0,1},{1,0},{2,3},{3,2},{4,5},{5,4},{6,7},{7,6},{8,9},{9,8},{10,11... | collective-permute-start | bytes 2654216 | tf_op jit(solution)/shard_map/ppermute | solution.py:13
  117.3 8.6 %collective-permute-start.10 = (bf16[12,8,4,256]{3,0,2,1:T(8,128)(2,1)}, bf16[12,8,4,256]{3,0,2,1:T(8,128)(2,1)S(1)}, u32[]{:S(2)}, u32[]{:S(2)}) collective-permute-start(bf16[12,8,4,256]{3,0,2,1:T(8,128)(2,1)} %collective-permute-done.9), channel_id=1, source_target_pairs={{0,4},{1,5},{2,6},{3,7},{4,0},{5,1},{6,2},{7,3},{8,12},{9,13},{10,... | collective-permute-start | bytes 589832 | tf_op jit(solution)/shard_map/ppermute | solution.py:13
  118.4 8.1 %copy-start.10 = (bf16[12,4,32,256]{3,0,2,1:T(8,128)(2,1)S(1)}, bf16[12,4,32,256]{3,0,2,1:T(8,128)(2,1)}, u32[]{:S(2)}) copy-start(bf16[12,4,32,256]{3,0,2,1:T(8,128)(2,1)} %get-tuple-element.54) | copy-start | bytes 2359300
  125.9 7.7 %collective-permute-start.11 = (bf16[12,8,4,256]{3,0,2,1:T(8,128)(2,1)S(1)}, bf16[12,8,4,256]{3,0,2,1:T(8,128)(2,1)S(1)}, u32[]{:S(2)}, u32[]{:S(2)}) collective-permute-start(bf16[12,8,4,256]{3,0,2,1:T(8,128)(2,1)S(1)} %collective-permute-done.10), channel_id=1, source_target_pairs={{0,8},{1,9},{2,10},{3,11},{4,12},{5,13},{6,14},{7,15},{8,0},{9,1},... | collective-permute-start | bytes 589832 | tf_op jit(solution)/shard_map/ppermute | solution.py:13
  126.5 9.4 %copy-start.11 = (bf16[12,4,32,256]{3,0,2,1:T(8,128)(2,1)S(1)}, bf16[12,4,32,256]{3,0,2,1:T(8,128)(2,1)}, u32[]{:S(2)}) copy-start(bf16[12,4,32,256]{3,0,2,1:T(8,128)(2,1)} %get-tuple-element.39) | copy-start | bytes 2359300
  133.6 15.8 %collective-permute-start.12 = (bf16[12,8,4,256]{3,0,2,1:T(8,128)(2,1)S(1)}, bf16[12,8,4,256]{3,0,2,1:T(8,128)(2,1)S(1)}, u32[]{:S(2)}, u32[]{:S(2)}) collective-permute-start(bf16[12,8,4,256]{3,0,2,1:T(8,128)(2,1)S(1)} %collective-permute-done.11), channel_id=1, source_target_pairs={{0,16},{1,17},{2,18},{3,19},{4,20},{5,21},{6,22},{7,23},{8,24},{9,... | collective-permute-start | bytes 589832 | tf_op jit(solution)/shard_map/ppermute | solution.py:13
  151.7 3.9 %slice-start = ((s8[4718592]{0:T(1024)(128)(4,1)}), s8[4194304]{0:T(1024)(128)(4,1)S(1)}, s32[]{:S(2)}) async-start(s8[4718592]{0:T(1024)(128)(4,1)} %bitcast.111), calls=%async_computation.1 | async-start | bytes 8388608
  151.7 4.0 %slice-start.1 = ((s8[4718592]{0:T(1024)(128)(4,1)}), s8[524288]{0:T(1024)(128)(4,1)S(1)}, s32[]{:S(2)}) async-start(s8[4718592]{0:T(1024)(128)(4,1)} %bitcast.111), calls=%async_computation.2 | async-start | bytes 1048576
  158.7 48.6 %collective-permute-start.15 = (bf16[12,2,36,256]{3,1,2,0:T(2,128)(2,1)}, bf16[12,2,36,256]{3,1,2,0:T(2,128)(2,1)S(1)}, u32[]{:S(2)}, u32[]{:S(2)}) collective-permute-start(bf16[12,2,36,256]{3,1,2,0:T(2,128)(2,1)} %copy.103), channel_id=1, source_target_pairs={{2,0},{4,2},{6,4},{8,6},{10,8},{12,10},{14,12},{16,14},{18,16},{20... | collective-permute-start | bytes 1327112 | tf_op jit(solution)/shard_map/ppermute | solution.py:25
  164.1 43.3 %collective-permute-start.14 = (bf16[12,2,36,256]{3,1,2,0:T(2,128)(2,1)}, bf16[12,2,36,256]{3,1,2,0:T(2,128)(2,1)}, u32[]{:S(2)}, u32[]{:S(2)}) collective-permute-start(bf16[12,2,36,256]{3,1,2,0:T(2,128)(2,1)} %copy.102), channel_id=1, source_target_pairs={{0,2},{2,4},{4,6},{6,8},{8,10},{10,12},{12,14},{14,16},{16,18},{18... | collective-permute-start | bytes 1327112 | tf_op jit(solution)/shard_map/ppermute | solution.py:22
  209.4 66.4 %collective-permute-start.16 = (bf16[12,12,2,256]{3,0,2,1:T(8,128)(2,1)}, bf16[12,12,2,256]{3,0,2,1:T(8,128)(2,1)}, u32[]{:S(2)}, u32[]{:S(2)}) collective-permute-start(bf16[12,12,2,256]{3,0,2,1:T(8,128)(2,1)} %get-tuple-element.26), channel_id=1, source_target_pairs={{0,1},{1,0},{2,3},{3,2},{4,5},{5,4},{6,7},{7,6},{8,9},{9,8},{10,11... | collective-permute-start | bytes 442376 | tf_op jit(solution)/shard_map/ppermute | solution.py:22
  211.6 64.1 %collective-permute-start.17 = (bf16[12,12,2,256]{3,0,2,1:T(8,128)(2,1)}, bf16[12,12,2,256]{3,0,2,1:T(8,128)(2,1)}, u32[]{:S(2)}, u32[]{:S(2)}) collective-permute-start(bf16[12,12,2,256]{3,0,2,1:T(8,128)(2,1)} %get-tuple-element.27), channel_id=1, source_target_pairs={{1,0},{0,1},{3,2},{2,3},{5,4},{4,5},{7,6},{6,7},{9,8},{8,9},{11,10... | collective-permute-start | bytes 442376 | tf_op jit(solution)/shard_map/ppermute | solution.py:25
  (12 other events, 17.8 us)
Sparse Core Ops, SparseCore 0:
  137.3 135.0 all-reduce.7
where the time goes:
time: 289 us; the launch traced here: 288 us
  waiting for transfers between devices  118 us (41%)
  blocking collectives  42.6 us (15%)
  local copies, waits for them, and re-layouts  37.7 us (13%)
  starting transfers between devices  28.4 us (10%)
  matrix products  24.5 us (8%)
  other arithmetic  23.1 us (8%)
  between operations  14.6 us (5%)
    psum x1, waiting for transfers between devices, local(): lax.psum((kernel_local, bias_local), ('frow', 'fcol'))  60.8 us
    ppermute x10, waiting for transfers between devices, from_partner(): lax.ppermute(value, axis, [(i, i ^ 1 << distance) for i in range(lax.axis...  44.4 us
    psum x1, blocking collectives, local(): lax.psum((kernel_local, bias_local), ('frow', 'fcol'))  42.6 us
    ppermute x10, starting transfers between devices, from_partner(): lax.ppermute(value, axis, [(i, i ^ 1 << distance) for i in range(lax.axis...  14.2 us
    unnamed x59, local copies, waits for them, and re-layouts  11.3 us
    ppermute x4, starting transfers between devices, with_halo(): lax.ppermute(lax.slice_in_dim(block, 0, width, axis=dim), axis, backward)  11.2 us
    ppermute x4, waiting for transfers between devices, with_halo(): lax.ppermute(lax.slice_in_dim(block, block.shape[dim] - width, None, axis...  9.43 us
    conv_general_dilated x1, matrix products, local(): lax.conv_general_dilated(preactivation_gradient, rotated_strip, (1, 1), (...  8.28 us
  transfers between devices with their start and end apart: 19, of which 10 were waited for; matrix products, arithmetic and copies ran while one was open for 13% of the time, Pallas kernels for 0%

commit v1 on v0

--- a/solution.py
+++ b/solution.py
@@ -189,7 +189,7 @@
             )
     kernel_local = jnp.stack(tap_list, 0).reshape(kernel.shape)
     bias_local = jnp.sum(preactivation_gradient.astype(jnp.float32), axis=(0, 1, 2))
-    kernel_total, bias_total = lax.psum((kernel_local, bias_local), ("frow", "fcol"))
+    kernel_total, bias_total = lax.psum(lax.psum((kernel_local, bias_local), "fcol"), "frow")
     scale = 1.0 / math.sqrt(
         face_count * tile_rows * lax.axis_size("frow") * tile_cols * lax.axis_size("fcol")
     )

time: 289 us -> 328 us (1.13)
  waiting for transfers between devices: 118 us -> 160 us
  blocking collectives: 42.6 us -> 38.1 us
    psum x1 -> x2, waiting for transfers between devices: 60.8 us -> 99.7 us  [the longest x1 96.6 us: local(): lax.psum(lax.psum((kernel_local, bias_local), 'fcol'), 'frow')]
    psum x1 -> x2, blocking collectives: 42.6 us -> 38.1 us  [the longest x1 33.2 us: local(): lax.psum(lax.psum((kernel_local, bias_local), 'fcol'), 'frow')]
    unnamed x59 -> x63, local copies, waits for them, and re-layouts: 11.3 us -> 11.6 us
  transfers between devices with their start and end apart: 19 -> 20, of which waited for: 10 -> 13; matrix products, arithmetic and copies ran while one was open for 13% -> 12% of each run, Pallas kernels for 0% -> 0%
where the time goes in v1:
time: 328 us; the launch traced here: 327 us
  waiting for transfers between devices  160 us (49%)
  blocking collectives  38.1 us (12%)
  local copies, waits for them, and re-layouts  37.9 us (12%)
  starting transfers between devices  27.3 us (8%)
  other arithmetic  25 us (8%)
  matrix products  24.5 us (7%)
  between operations  14.6 us (4%)
    psum x1, waiting for transfers between devices, local(): lax.psum(lax.psum((kernel_local, bias_local), 'fcol'), 'frow')  96.6 us
    ppermute x10, waiting for transfers between devices, from_partner(): lax.ppermute(value, axis, [(i, i ^ 1 << distance) for i in range(lax.axis...  42.1 us
    psum x1, blocking collectives, local(): lax.psum(lax.psum((kernel_local, bias_local), 'fcol'), 'frow')  33.2 us
    ppermute x10, starting transfers between devices, from_partner(): lax.ppermute(value, axis, [(i, i ^ 1 << distance) for i in range(lax.axis...  14 us
    ppermute x4, waiting for transfers between devices, with_halo(): lax.ppermute(lax.slice_in_dim(block, block.shape[dim] - width, None, axis...  12.6 us
    unnamed x63, local copies, waits for them, and re-layouts  11.6 us
    ppermute x4, starting transfers between devices, with_halo(): lax.ppermute(lax.slice_in_dim(block, 0, width, axis=dim), axis, backward)  11.2 us
    conv_general_dilated x1, matrix products, local(): lax.conv_general_dilated(preactivation_gradient, rotated_strip, (1, 1), (...  8.29 us
  transfers between devices with their start and end apart: 20, of which 13 were waited for; matrix products, arithmetic and copies ran while one was open for 12% of the time, Pallas kernels for 0%

profile of v1, /device:TPU:0, one launch (start us, length us, event | category | flops | bytes accessed | tf_op | source)
XLA Modules:
  0.0 327.4 jit_solution(18216742681642354880)
XLA Ops:
  9.5 5.1 %collective-permute-start.1 = (bf16[12,2,32,256]{3,0,2,1:T(8,128)(2,1)S(1)}, bf16[12,2,32,256]{3,0,2,1:T(8,128)(2,1)S(1)}, u32[]{:S(2)}, u32[]{:S(2)}) collective-permute-start(bf16[12,2,32,256]{3,0,2,1:T(8,128)(2,1)S(1)} %copy.171), channel_id=1, source_target_pairs={{2,0},{4,2},{6,4},{8,6},{10,8},{12,10},{14,12},{16,14},{18,16},{20... | collective-permute-start | bytes 1179656 | tf_op jit(solution)/shard_map/ppermute | solution.py:25
  14.6 6.8 %collective-permute-done = bf16[12,2,32,256]{3,0,2,1:T(8,128)(2,1)} collective-permute-done((bf16[12,2,32,256]{3,0,2,1:T(8,128)(2,1)S(1)}, bf16[12,2,32,256]{3,0,2,1:T(8,128)(2,1)}, u32[]{:S(2)}, u32[]{:S(2)}) %collective-permute-start) | collective-permute-done | bytes 393248 | tf_op jit(solution)/shard_map/ppermute | solution.py:22
  24.3 2.0 collective-permute-start.3
  26.5 2.9 collective-permute-done.3
  29.4 2.8 collective-permute-done.2
  42.2 6.7 %collective-permute-done.5 = bf16[12,8,4,256]{3,0,2,1:T(8,128)(2,1)S(1)} collective-permute-done((bf16[12,8,4,256]{3,0,2,1:T(8,128)(2,1)S(1)}, bf16[12,8,4,256]{3,0,2,1:T(8,128)(2,1)S(1)}, u32[]{:S(2)}, u32[]{:S(2)}) %collective-permute-start.5) | collective-permute-done | bytes 196640 | tf_op jit(solution)/shard_map/ppermute | solution.py:13
  50.4 6.3 %collective-permute-done.6 = bf16[12,8,4,256]{3,0,2,1:T(8,128)(2,1)S(1)} collective-permute-done((bf16[12,8,4,256]{3,0,2,1:T(8,128)(2,1)S(1)}, bf16[12,8,4,256]{3,0,2,1:T(8,128)(2,1)S(1)}, u32[]{:S(2)}, u32[]{:S(2)}) %collective-permute-start.6) | collective-permute-done | bytes 196640 | tf_op jit(solution)/shard_map/ppermute | solution.py:13
  56.7 2.8 collective-permute-start.7
  63.4 7.3 %collective-permute-done.7 = bf16[12,8,4,256]{3,0,2,1:T(8,128)(2,1)} collective-permute-done((bf16[12,8,4,256]{3,0,2,1:T(8,128)(2,1)S(1)}, bf16[12,8,4,256]{3,0,2,1:T(8,128)(2,1)}, u32[]{:S(2)}, u32[]{:S(2)}) %collective-permute-start.7) | collective-permute-done | bytes 196640 | tf_op jit(solution)/shard_map/ppermute | solution.py:13
  72.4 3.0 fusion.111
  82.0 2.7 broadcast_select_fusion.1
  87.5 2.1 pad_maximum_fusion.5
  89.6 2.8 fusion.5
  92.4 2.6 convert_reduce_fusion
  95.0 8.3 %fusion.115 = (f32[12,8,36,256]{3,0,2,1:T(8,128)}, bf16[12,8,36,256]{3,0,2,1:T(8,128)(2,1)S(1)}) fusion(bf16[3,3,256,256]{3,2,1,0:T(8,128)(2,1)S(1)} %copy-done, bf16[12,4,32,256]{3,2,1,0:T(8,128)(2,1)S(1)} %get-tuple-element.21), kind=kOutput, calls=%fused_computation.189 | convolution fusion | flops 1813708800 | bytes 7274496 | tf_op jit(solution)/shard_map/conv_general_dilated | solution.py:200
  103.7 2.6 fusion.60
  111.1 2.0 fusion.108
  121.2 6.3 %collective-permute-done.10 = bf16[12,8,4,256]{3,0,2,1:T(8,128)(2,1)S(1)} collective-permute-done((bf16[12,8,4,256]{3,0,2,1:T(8,128)(2,1)}, bf16[12,8,4,256]{3,0,2,1:T(8,128)(2,1)S(1)}, u32[]{:S(2)}, u32[]{:S(2)}) %collective-permute-start.10) | collective-permute-done | bytes 196640 | tf_op jit(solution)/shard_map/ppermute | solution.py:13
  129.3 5.9 %collective-permute-done.11 = bf16[12,8,4,256]{3,0,2,1:T(8,128)(2,1)S(1)} collective-permute-done((bf16[12,8,4,256]{3,0,2,1:T(8,128)(2,1)S(1)}, bf16[12,8,4,256]{3,0,2,1:T(8,128)(2,1)S(1)}, u32[]{:S(2)}, u32[]{:S(2)}) %collective-permute-start.11) | collective-permute-done | bytes 196640 | tf_op jit(solution)/shard_map/ppermute | solution.py:13
  135.2 2.4 collective-permute-start.12
  138.9 9.8 %collective-permute-done.12 = bf16[12,8,4,256]{3,0,2,1:T(8,128)(2,1)S(1)} collective-permute-done((bf16[12,8,4,256]{3,0,2,1:T(8,128)(2,1)S(1)}, bf16[12,8,4,256]{3,0,2,1:T(8,128)(2,1)S(1)}, u32[]{:S(2)}, u32[]{:S(2)}) %collective-permute-start.12) | collective-permute-done | bytes 196640 | tf_op jit(solution)/shard_map/ppermute | solution.py:13
  148.7 2.2 fusion.110
  151.0 3.5 %slice_select_fusion.3 = (f32[12,2,36,256]{3,0,2,1:T(8,128)S(1)}, f32[12,2,36,256]{3,0,2,1:T(8,128)S(1)}, f32[12,2,36,256]{3,0,2,1:T(8,128)S(1)}) fusion(f32[12,8,36,256]{3,0,2,1:T(8,128)} %get-tuple-element.70, f32[48,2,36,256]{3,0,2,1:T(8,128)} %fusion.60, bf16[12,2,36,256]{3,1,2,0:T(2,128)(2,1)S(1)} %get-tuple-element.57, pred[]{:T(512)S(6)} %eq.57, ...), kind=kLoop, calls=%fused_computation.53 | loop fusion | flops 884736 | bytes 6635522 | tf_op jit(solution)/shard_map/jit(_where)/select_n | solution.py:243
  158.4 3.6 %collective-permute-start.15 = (bf16[12,2,36,256]{3,1,2,0:T(2,128)(2,1)}, bf16[12,2,36,256]{3,1,2,0:T(2,128)(2,1)S(1)}, u32[]{:S(2)}, u32[]{:S(2)}) collective-permute-start(bf16[12,2,36,256]{3,1,2,0:T(2,128)(2,1)} %copy.103), channel_id=1, source_target_pairs={{2,0},{4,2},{6,4},{8,6},{10,8},{12,10},{14,12},{16,14},{18,16},{20... | collective-permute-start | bytes 1327112 | tf_op jit(solution)/shard_map/ppermute | solution.py:25
  163.2 5.0 %psum.30 = f32[256]{0:T(256)S(1)} all-reduce(f32[256]{0:T(256)S(1)} %get-tuple-element.20), channel_id=1, replica_groups=mesh['frow'=16,'fcol'=2] {'fcol'}, use_global_device_ids=true, to_apply=%region_3.4 | all-reduce | flops 256 | bytes 2048 | tf_op jit(solution)/shard_map/psum | solution.py:192
  168.2 33.2 %psum.31 = f32[256]{0:T(256)S(1)} all-reduce(f32[256]{0:T(256)S(1)} %psum.30), channel_id=1, replica_groups=mesh['frow'=16,'fcol'=2] {'frow'}, use_global_device_ids=true, to_apply=%region_4.5 | all-reduce | flops 256 | bytes 2048 | tf_op jit(solution)/shard_map/psum | solution.py:192
  206.0 3.1 all-reduce.9.cloned.1.call-done
  209.1 3.1 collective-permute-done.16
  212.2 2.6 collective-permute-done.17
  214.8 2.9 maximum_convert_fusion
  220.7 96.6 %all-reduce.11.cloned.1.call-done = f32[3,3,256,256]{3,2,1,0:T(8,128)} async-done(((f32[3,3,256,256]{3,2,1,0:T(8,128)}), f32[3,3,256,256]{3,2,1,0:T(8,128)}) %all-reduce.11.cloned.1.call-update) | async-done | bytes 2359312 | tf_op jit(solution)/shard_map/psum | solution.py:192
  317.3 3.3 broadcast_multiply_fusion
  (150 shorter events, 61.1 us)
Async XLA Ops:
  7.2 82.4 %copy-start = (bf16[3,3,256,256]{3,2,1,0:T(8,128)(2,1)S(1)}, bf16[3,3,256,256]{3,2,1,0:T(8,128)(2,1)}, u32[]{:S(2)}) copy-start(bf16[3,3,256,256]{3,2,1,0:T(8,128)(2,1)} %param.6) | copy-start | bytes 3538948
  7.2 15.3 %copy-start.3 = (bf16[12,4,32,256]{3,2,1,0:T(8,128)(2,1)S(1)}, bf16[12,4,32,256]{3,2,1,0:T(8,128)(2,1)}, u32[]{:S(2)}) copy-start(bf16[12,4,32,256]{3,2,1,0:T(8,128)(2,1)} %param.5) | copy-start | bytes 2359300
  7.2 201.9 %all-reduce.9.cloned.1.call-start = ((), (), s32[]{:S(2)}) async-start(), calls=%async_computation | async-start | bytes 4718592 | tf_op jit(solution)/shard_map/psum | solution.py:192
  8.8 12.6 %collective-permute-start = (bf16[12,2,32,256]{3,0,2,1:T(8,128)(2,1)S(1)}, bf16[12,2,32,256]{3,0,2,1:T(8,128)(2,1)}, u32[]{:S(2)}, u32[]{:S(2)}) collective-permute-start(bf16[12,2,32,256]{3,0,2,1:T(8,128)(2,1)S(1)} %copy.170), channel_id=1, source_target_pairs={{0,2},{2,4},{4,6},{6,8},{8,10},{10,12},{12,14},{14,16},{16,18},{18... | collective-permute-start | bytes 1179656 | tf_op jit(solution)/shard_map/ppermute | solution.py:22
  9.5 16.9 %copy-start.19 = (s32[12,4,3]{0,1,2:T(4,128)S(1)}, s32[12,4,3]{0,1,2:T(4,128)}, u32[]{:S(2)}) copy-start(s32[12,4,3]{0,1,2:T(4,128)} %param.9) | copy-start | bytes 1732
  9.5 13.4 %collective-permute-start.1 = (bf16[12,2,32,256]{3,0,2,1:T(8,128)(2,1)S(1)}, bf16[12,2,32,256]{3,0,2,1:T(8,128)(2,1)S(1)}, u32[]{:S(2)}, u32[]{:S(2)}) collective-permute-start(bf16[12,2,32,256]{3,0,2,1:T(8,128)(2,1)S(1)} %copy.171), channel_id=1, source_target_pairs={{2,0},{4,2},{6,4},{8,6},{10,8},{12,10},{14,12},{16,14},{18,16},{20... | collective-permute-start | bytes 1179656 | tf_op jit(solution)/shard_map/ppermute | solution.py:25
  24.3 5.0 %collective-permute-start.3 = (bf16[12,8,2,256]{3,0,2,1:T(8,128)(2,1)S(1)}, bf16[12,8,2,256]{3,0,2,1:T(8,128)(2,1)S(1)}, u32[]{:S(2)}, u32[]{:S(2)}) collective-permute-start(bf16[12,8,2,256]{3,0,2,1:T(8,128)(2,1)S(1)} %get-tuple-element.49), channel_id=1, source_target_pairs={{1,0},{0,1},{3,2},{2,3},{5,4},{4,5},{7,6},{6,7},{9,8},{8,9},{11,10... | collective-permute-start | bytes 294920 | tf_op jit(solution)/shard_map/ppermute | solution.py:25
  26.3 5.8 %collective-permute-start.2 = (bf16[12,8,2,256]{3,0,2,1:T(8,128)(2,1)S(1)}, bf16[12,8,2,256]{3,0,2,1:T(8,128)(2,1)S(1)}, u32[]{:S(2)}, u32[]{:S(2)}) collective-permute-start(bf16[12,8,2,256]{3,0,2,1:T(8,128)(2,1)S(1)} %get-tuple-element.51), channel_id=1, source_target_pairs={{0,1},{1,0},{2,3},{3,2},{4,5},{5,4},{6,7},{7,6},{8,9},{9,8},{10,11... | collective-permute-start | bytes 294920 | tf_op jit(solution)/shard_map/ppermute | solution.py:22
  32.2 8.2 %collective-permute-start.4 = (bf16[12,8,4,256]{3,0,2,1:T(8,128)(2,1)S(1)}, bf16[12,8,4,256]{3,0,2,1:T(8,128)(2,1)S(1)}, u32[]{:S(2)}, u32[]{:S(2)}) collective-permute-start(bf16[12,8,4,256]{3,0,2,1:T(8,128)(2,1)S(1)} %pad_maximum_fusion.12), channel_id=1, source_target_pairs={{0,2},{1,3},{2,0},{3,1},{4,6},{5,7},{6,4},{7,5},{8,10},{9,11},{10,... | collective-permute-start | bytes 589832 | tf_op jit(solution)/shard_map/ppermute | solution.py:13
  36.1 4.3 %copy-start.7 = (bf16[12,2,36,256]{3,0,2,1:T(8,128)(2,1)}, bf16[12,2,36,256]{3,0,2,1:T(8,128)(2,1)S(1)}, u32[]{:S(2)}) copy-start(bf16[12,2,36,256]{3,0,2,1:T(8,128)(2,1)S(1)} %get-tuple-element.37) | copy-start | bytes 1327108
  39.0 33.3 %collective-permute-start.8 = (bf16[12,4,36,256]{3,1,2,0:T(4,128)(2,1)}, bf16[12,4,36,256]{3,1,2,0:T(4,128)(2,1)}, u32[]{:S(2)}, u32[]{:S(2)}) collective-permute-start(bf16[12,4,36,256]{3,1,2,0:T(4,128)(2,1)} %copy.94), channel_id=1, source_target_pairs={{0,1},{1,0},{2,3},{3,2},{4,5},{5,4},{6,7},{7,6},{8,9},{9,8},{10,11... | collective-permute-start | bytes 2654216 | tf_op jit(solution)/shard_map/ppermute | solution.py:13
  40.4 8.4 %collective-permute-start.5 = (bf16[12,8,4,256]{3,0,2,1:T(8,128)(2,1)S(1)}, bf16[12,8,4,256]{3,0,2,1:T(8,128)(2,1)S(1)}, u32[]{:S(2)}, u32[]{:S(2)}) collective-permute-start(bf16[12,8,4,256]{3,0,2,1:T(8,128)(2,1)S(1)} %collective-permute-done.4), channel_id=1, source_target_pairs={{0,4},{1,5},{2,6},{3,7},{4,0},{5,1},{6,2},{7,3},{8,12},{9,13},{10,... | collective-permute-start | bytes 589832 | tf_op jit(solution)/shard_map/ppermute | solution.py:13
  42.2 39.9 %copy-start.23 = (pred[36]{0:T(512)(128)(4,1)}, pred[36]{0:T(512)(128)(4,1)S(1)}, u32[]{:S(2)}) copy-start(pred[36]{0:T(512)(128)(4,1)S(1)} %or_not_fusion) | copy-start | bytes 112
  48.9 7.9 %collective-permute-start.6 = (bf16[12,8,4,256]{3,0,2,1:T(8,128)(2,1)S(1)}, bf16[12,8,4,256]{3,0,2,1:T(8,128)(2,1)S(1)}, u32[]{:S(2)}, u32[]{:S(2)}) collective-permute-start(bf16[12,8,4,256]{3,0,2,1:T(8,128)(2,1)S(1)} %collective-permute-done.5), channel_id=1, source_target_pairs={{0,8},{1,9},{2,10},{3,11},{4,12},{5,13},{6,14},{7,15},{8,0},{9,1},... | collective-permute-start | bytes 589832 | tf_op jit(solution)/shard_map/ppermute | solution.py:13
  56.7 14.0 %collective-permute-start.7 = (bf16[12,8,4,256]{3,0,2,1:T(8,128)(2,1)S(1)}, bf16[12,8,4,256]{3,0,2,1:T(8,128)(2,1)}, u32[]{:S(2)}, u32[]{:S(2)}) collective-permute-start(bf16[12,8,4,256]{3,0,2,1:T(8,128)(2,1)S(1)} %collective-permute-done.6), channel_id=1, source_target_pairs={{0,16},{1,17},{2,18},{3,19},{4,20},{5,21},{6,22},{7,23},{8,24},{9,... | collective-permute-start | bytes 589832 | tf_op jit(solution)/shard_map/ppermute | solution.py:13
  95.0 8.7 %copy-start.24 = (pred[36]{0:T(512)(128)(4,1)S(1)}, pred[36]{0:T(512)(128)(4,1)}, u32[]{:S(2)}) copy-start(pred[36]{0:T(512)(128)(4,1)} %copy-done.23) | copy-start | bytes 112
  111.1 7.7 %collective-permute-start.9 = (bf16[12,8,4,256]{3,0,2,1:T(8,128)(2,1)}, bf16[12,8,4,256]{3,0,2,1:T(8,128)(2,1)}, u32[]{:S(2)}, u32[]{:S(2)}) collective-permute-start(bf16[12,8,4,256]{3,0,2,1:T(8,128)(2,1)} %pad_maximum_fusion.13), channel_id=1, source_target_pairs={{0,2},{1,3},{2,0},{3,1},{4,6},{5,7},{6,4},{7,5},{8,10},{9,11},{10,... | collective-permute-start | bytes 589832 | tf_op jit(solution)/shard_map/ppermute | solution.py:13
  117.0 31.8 %collective-permute-start.13 = (bf16[12,4,36,256]{3,1,2,0:T(4,128)(2,1)}, bf16[12,4,36,256]{3,1,2,0:T(4,128)(2,1)}, u32[]{:S(2)}, u32[]{:S(2)}) collective-permute-start(bf16[12,4,36,256]{3,1,2,0:T(4,128)(2,1)} %copy.99), channel_id=1, source_target_pairs={{0,1},{1,0},{2,3},{3,2},{4,5},{5,4},{6,7},{7,6},{8,9},{9,8},{10,11... | collective-permute-start | bytes 2654216 | tf_op jit(solution)/shard_map/ppermute | solution.py:13
  118.8 8.6 %collective-permute-start.10 = (bf16[12,8,4,256]{3,0,2,1:T(8,128)(2,1)}, bf16[12,8,4,256]{3,0,2,1:T(8,128)(2,1)S(1)}, u32[]{:S(2)}, u32[]{:S(2)}) collective-permute-start(bf16[12,8,4,256]{3,0,2,1:T(8,128)(2,1)} %collective-permute-done.9), channel_id=1, source_target_pairs={{0,4},{1,5},{2,6},{3,7},{4,0},{5,1},{6,2},{7,3},{8,12},{9,13},{10,... | collective-permute-start | bytes 589832 | tf_op jit(solution)/shard_map/ppermute | solution.py:13
  119.9 8.2 %copy-start.12 = (bf16[12,4,32,256]{3,0,2,1:T(8,128)(2,1)S(1)}, bf16[12,4,32,256]{3,0,2,1:T(8,128)(2,1)}, u32[]{:S(2)}) copy-start(bf16[12,4,32,256]{3,0,2,1:T(8,128)(2,1)} %get-tuple-element.54) | copy-start | bytes 2359300
  127.5 7.7 %collective-permute-start.11 = (bf16[12,8,4,256]{3,0,2,1:T(8,128)(2,1)S(1)}, bf16[12,8,4,256]{3,0,2,1:T(8,128)(2,1)S(1)}, u32[]{:S(2)}, u32[]{:S(2)}) collective-permute-start(bf16[12,8,4,256]{3,0,2,1:T(8,128)(2,1)S(1)} %collective-permute-done.10), channel_id=1, source_target_pairs={{0,8},{1,9},{2,10},{3,11},{4,12},{5,13},{6,14},{7,15},{8,0},{9,1},... | collective-permute-start | bytes 589832 | tf_op jit(solution)/shard_map/ppermute | solution.py:13
  128.1 9.5 %copy-start.13 = (bf16[12,4,32,256]{3,0,2,1:T(8,128)(2,1)S(1)}, bf16[12,4,32,256]{3,0,2,1:T(8,128)(2,1)}, u32[]{:S(2)}) copy-start(bf16[12,4,32,256]{3,0,2,1:T(8,128)(2,1)} %get-tuple-element.39) | copy-start | bytes 2359300
  135.2 13.5 %collective-permute-start.12 = (bf16[12,8,4,256]{3,0,2,1:T(8,128)(2,1)S(1)}, bf16[12,8,4,256]{3,0,2,1:T(8,128)(2,1)S(1)}, u32[]{:S(2)}, u32[]{:S(2)}) collective-permute-start(bf16[12,8,4,256]{3,0,2,1:T(8,128)(2,1)S(1)} %collective-permute-done.11), channel_id=1, source_target_pairs={{0,16},{1,17},{2,18},{3,19},{4,20},{5,21},{6,22},{7,23},{8,24},{9,... | collective-permute-start | bytes 589832 | tf_op jit(solution)/shard_map/ppermute | solution.py:13
  138.8 178.5 %all-reduce.11.cloned.1.call-start = ((), (), s32[]{:S(2)}) async-start(), calls=%async_computation.1 | async-start | bytes 4718592 | tf_op jit(solution)/shard_map/psum | solution.py:192
  151.0 4.0 %slice-start.1 = ((s8[4718592]{0:T(1024)(128)(4,1)}), s8[524288]{0:T(1024)(128)(4,1)S(1)}, s32[]{:S(2)}) async-start(s8[4718592]{0:T(1024)(128)(4,1)} %bitcast.111), calls=%async_computation.3 | async-start | bytes 1048576
  157.2 45.4 %copy-start.9 = (bf16[12,8,2,256]{3,0,2,1:T(8,128)(2,1)S(1)}, bf16[12,8,2,256]{3,0,2,1:T(8,128)(2,1)}, u32[]{:S(2)}) copy-start(bf16[12,8,2,256]{3,0,2,1:T(8,128)(2,1)} %copy-done.8) | copy-start | bytes 294916
  157.2 45.4 %copy-start.11 = (bf16[12,8,2,256]{3,0,2,1:T(8,128)(2,1)S(1)}, bf16[12,8,2,256]{3,0,2,1:T(8,128)(2,1)}, u32[]{:S(2)}) copy-start(bf16[12,8,2,256]{3,0,2,1:T(8,128)(2,1)} %copy-done.10) | copy-start | bytes 294916
  158.4 42.9 %collective-permute-start.15 = (bf16[12,2,36,256]{3,1,2,0:T(2,128)(2,1)}, bf16[12,2,36,256]{3,1,2,0:T(2,128)(2,1)S(1)}, u32[]{:S(2)}, u32[]{:S(2)}) collective-permute-start(bf16[12,2,36,256]{3,1,2,0:T(2,128)(2,1)} %copy.103), channel_id=1, source_target_pairs={{2,0},{4,2},{6,4},{8,6},{10,8},{12,10},{14,12},{16,14},{18,16},{20... | collective-permute-start | bytes 1327112 | tf_op jit(solution)/shard_map/ppermute | solution.py:25
  163.2 38.2 %collective-permute-start.14 = (bf16[12,2,36,256]{3,1,2,0:T(2,128)(2,1)}, bf16[12,2,36,256]{3,1,2,0:T(2,128)(2,1)}, u32[]{:S(2)}, u32[]{:S(2)}) collective-permute-start(bf16[12,2,36,256]{3,1,2,0:T(2,128)(2,1)} %copy.102), channel_id=1, source_target_pairs={{0,2},{2,4},{4,6},{6,8},{8,10},{10,12},{12,14},{14,16},{16,18},{18... | collective-permute-start | bytes 1327112 | tf_op jit(solution)/shard_map/ppermute | solution.py:22
  203.4 8.8 %collective-permute-start.16 = (bf16[12,12,2,256]{3,0,2,1:T(8,128)(2,1)}, bf16[12,12,2,256]{3,0,2,1:T(8,128)(2,1)}, u32[]{:S(2)}, u32[]{:S(2)}) collective-permute-start(bf16[12,12,2,256]{3,0,2,1:T(8,128)(2,1)} %get-tuple-element.26), channel_id=1, source_target_pairs={{0,1},{1,0},{2,3},{3,2},{4,5},{5,4},{6,7},{7,6},{8,9},{9,8},{10,11... | collective-permute-start | bytes 442376 | tf_op jit(solution)/shard_map/ppermute | solution.py:22
  204.8 10.0 %collective-permute-start.17 = (bf16[12,12,2,256]{3,0,2,1:T(8,128)(2,1)}, bf16[12,12,2,256]{3,0,2,1:T(8,128)(2,1)}, u32[]{:S(2)}, u32[]{:S(2)}) collective-permute-start(bf16[12,12,2,256]{3,0,2,1:T(8,128)(2,1)} %get-tuple-element.27), channel_id=1, source_target_pairs={{1,0},{0,1},{3,2},{2,3},{5,4},{4,5},{7,6},{6,7},{9,8},{8,9},{11,10... | collective-permute-start | bytes 442376 | tf_op jit(solution)/shard_map/ppermute | solution.py:25
  219.6 101.0 %copy-start.1 = (bf16[3,3,256,256]{3,2,1,0:T(8,128)(2,1)S(1)}, bf16[3,3,256,256]{3,2,1,0:T(8,128)(2,1)}, u32[]{:S(2)}) copy-start(bf16[3,3,256,256]{3,2,1,0:T(8,128)(2,1)} %param.6) | copy-start | bytes 3538948
  (15 other events, 27.1 us)
Sparse Core Ops, SparseCore 0:
  138.9 70.1 all-reduce.8
  213.1 104.1 all-reduce.10
